TPU v7x, 32 devices: a whole 2x2x4 slice. The times are simulated.
32 devices in a mesh: view: 4 (over y, core), bx: 2 (over x), by: 4 (over z).
Axes of the slice: x: 2, y: 2, z: 4, core: 2. Of those that a mesh axis runs over, the one named last changes fastest.
Arguments:
- estimate: float32 [2048, 512], P(('bx', 'by')), may hold values from 0.5 to 2
- recorded: float32 [4, 2048, 512], P('view', ('bx', 'by')), may hold values from 0.5 to 4
- resample: float32 [4, 4, 512, 512], P('view'), may hold values from 0 to 1, as said below
- psf_taps: float32 [4, 31], P('view'), may hold values from 0.2 to 1
- source_brick: int32 [4, 2048, 4], P('view', ('bx', 'by')), may hold values from 0 to 7, all different within a row; in each aligned block of 256 rows (0 to 255, 256 to 511, ..., all dimensions but the last counted through in order) at most 192 rows name the same one
- source_column: int32 [4, 2048, 4], P('view', ('bx', 'by')), may hold values from 0 to 255
Outputs:
- refined: float32 [2048, 512], P(('bx', 'by'))
Inputs may be any that keep to these rules, and one draw needn't show every extreme that they name: `source_brick`: in each view, the 4 bricks named for one column are different; among the columns of one brick, no joined brick is named more than 192 times, and some joined brick exactly 192 times. `resample`: all entries are nonnegative.
All inputs are finite; a program needn't handle non-finite values.
Results may differ from a plain program's by a relative error of at most 0.0001.
Values sent between devices are 32-bit elements; how exact they have to be, the bound alone decides.
A program may use at most 192 MiB of HBM per device.

v0:
```python
import jax
import jax.numpy as jnp
from jax import lax
from jax.sharding import PartitionSpec as P

ITERS = 2
precise = lax.Precision.HIGHEST


def blur_matrix(taps_row, column_len):
    spread = taps_row / jnp.sum(taps_row)
    tap_count = spread.shape[0]
    half_width = (tap_count - 1) // 2
    row_ids = lax.broadcasted_iota(jnp.int32, (column_len, column_len), 0)
    col_ids = lax.broadcasted_iota(jnp.int32, (column_len, column_len), 1)
    offset = row_ids - col_ids + half_width
    matrix = jnp.zeros((column_len, column_len), jnp.float32)
    for tap_number in range(tap_count):
        matrix = matrix + jnp.where(offset == tap_number, spread[tap_number], 0.0)
    return matrix


def per_device(estimate, recorded, resample, psf_taps, source_brick, source_column):
    bricks_x = lax.axis_size("bx")
    bricks_y = lax.axis_size("by")
    peer_count = bricks_x * bricks_y
    columns, column_len = estimate.shape
    sources = source_brick.shape[2]
    pair_count = columns * sources
    capacity = 3 * pair_count // (2 * peer_count)
    peer_ids = source_brick[0].reshape(pair_count)
    wanted = source_column[0].reshape(pair_count)
    branch_ids = lax.broadcasted_iota(jnp.int32, (columns, sources), 1).reshape(pair_count)
    peer_hits = (
        peer_ids[:, None] == lax.broadcasted_iota(jnp.int32, (pair_count, peer_count), 1)
    ).astype(jnp.int32)
    before = jnp.cumsum(peer_hits, axis=0) - peer_hits
    slot_rank = jnp.sum(before * peer_hits, axis=1)
    position = peer_ids * capacity + slot_rank
    request = (
        jnp.full((peer_count * capacity,), -1, jnp.int32)
        .at[position]
        .set(wanted * sources + branch_ids)
    )
    served = lax.all_to_all(
        request.reshape(peer_count, capacity), ("bx", "by"), split_axis=0, concat_axis=0, tiled=True
    )
    served = served.reshape(peer_count * capacity)
    owned_column = jnp.maximum(served, 0) // sources
    weights = resample[0]
    blurring = blur_matrix(psf_taps[0], column_len)
    unit_smeared = jnp.sum(blurring, axis=1)
    unit_back = jnp.einsum("b,kcb->kc", unit_smeared, weights, precision=precise)
    normalizer = None
    norm_local = None
    for sweep in range(ITERS):
        outgoing = estimate[owned_column]
        incoming = lax.all_to_all(
            outgoing.reshape(peer_count, capacity, column_len),
            ("bx", "by"),
            split_axis=0,
            concat_axis=0,
            tiled=True,
        )
        incoming = incoming.reshape(peer_count * capacity, column_len)
        pieces = incoming[position].reshape(columns, sources, column_len)
        forward = jnp.einsum("qkb,kbc->qc", pieces, weights, precision=precise)
        blurred = jnp.dot(forward, blurring, precision=precise)
        quotient = recorded[0] / blurred
        smeared = jnp.dot(quotient, blurring.T, precision=precise)
        contributions = jnp.einsum("qb,kcb->qkc", smeared, weights, precision=precise).reshape(
            pair_count, column_len
        )
        with_units = sweep == 0
        if with_units:
            unit_rows = jnp.broadcast_to(unit_back[None], (columns, sources, column_len)).reshape(
                pair_count, column_len
            )
            stacked = jnp.stack([contributions, unit_rows], axis=1)
        else:
            stacked = contributions[:, None, :]
        layers = stacked.shape[1]
        buffer = (
            jnp.zeros((peer_count * capacity, layers, column_len), jnp.float32)
            .at[position]
            .set(stacked)
        )
        returned = lax.all_to_all(
            buffer.reshape(peer_count, capacity, layers, column_len),
            ("bx", "by"),
            split_axis=0,
            concat_axis=0,
            tiled=True,
        )
        returned = returned.reshape(peer_count * capacity, layers, column_len)
        owned_sum = (
            jnp.zeros((columns, layers, column_len), jnp.float32).at[owned_column].add(returned)
        )
        correction_local = owned_sum[:, 0]
        if with_units:
            norm_local = owned_sum[:, 1]
        if sweep == 0:
            summands = jnp.stack([correction_local, norm_local])
        else:
            summands = correction_local[None]
        view_total = lax.psum(summands, "view")
        if sweep == 0:
            normalizer = view_total[1]
        estimate = estimate * (view_total[0] + 1.0) / (normalizer + 1.0)
    return estimate


def solution(mesh):
    return jax.shard_map(
        per_device,
        mesh=mesh,
        in_specs=(
            P(("bx", "by"), None),
            P("view", ("bx", "by"), None),
            P("view", None, None, None),
            P("view", None),
            P("view", ("bx", "by"), None),
            P("view", ("bx", "by"), None),
        ),
        out_specs=P(("bx", "by"), None),
        check_vma=False,
    )
```

profile of v0, /device:TPU:0, one launch (start us, length us, event | category | flops | bytes accessed | tf_op | source)
XLA Modules:
  0.0 890.5 jit_solution(9087115394177621034)
XLA Ops:
  17.0 13.6 %all_to_all.29 = s32[8,1,192]{2,1,0:T(1,128)S(1)} all-to-all(s32[8,1,192]{2,1,0:T(1,128)S(1)} %all_to_all.18), channel_id=1, replica_groups=mesh['view'=4,'bx'=2,'by'=4] {'bx','by'}, dimensions={0} | all-to-all | bytes 12288 | tf_op jit(solution)/shard_map/all_to_all | solution.py:45
  30.8 5.0 gather_fusion
  43.2 22.8 %fusion.58 = f32[512]{0:T(512)S(1)} fusion(f32[]{:T(128)} %bitcast.38, f32[]{:T(128)} %bitcast.37, f32[]{:T(128)} %bitcast.36, f32[]{:T(128)} %bitcast.35, f32[]{:T(128)} %bitcast.34, f32[]{:T(128)} %bitcast.33, f32[]{:T(128)} %bitcast.32, f32[]{:T(128)} %bitcast.31, f32[]{:T(128)} %bitcast.30, f32[]{:T(128)} %bitcast.29, f32[]{:T(128)} %bitcast.28, ...), kind=kLoop, calls=%fused_computation.73 | loop fusion | flops 24903168 | bytes 2172 | tf_op jit(solution)/shard_map/reduce_sum | solution.py:52
  66.0 5.7 fusion.4
  73.7 37.0 %all-to-all-done.1 = f32[8,192,512]{2,1,0:T(8,128)} async-done(((f32[8,192,512]{2,1,0:T(8,128)}), f32[8,192,512]{2,1,0:T(8,128)}, u32[]{:S(2)}, u32[]{:S(2)}) %all-to-all-start.1) | async-done | bytes 3145760 | tf_op jit(solution)/shard_map/all_to_all | solution.py:58
  110.7 5.9 gather_fusion.1
  118.3 7.2 fusion.14
  125.6 24.4 %convolution_divide_fusion.1 = f32[256,512]{1,0:T(8,128)S(1)} fusion(f32[256,512]{1,0:T(8,128)S(1)} %fusion.14, f32[1,256,512]{2,1,0:T(8,128)S(1)} %copy-done.5, f32[]{:T(128)} %bitcast.38, f32[]{:T(128)} %bitcast.37, f32[]{:T(128)} %bitcast.36, f32[]{:T(128)} %bitcast.35, f32[]{:T(128)} %bitcast.34, f32[]{:T(128)} %bitcast.33, f32[]{:T(128)} %bitcast.32, ...), kind=kOutput, calls=%fused_computation.25 | convolution fusion | flops 830078976 | bytes 1572988 | tf_op jit(solution)/shard_map/dot_general | solution.py:68
  150.0 25.1 %convolution_bitcast_fusion.1 = f32[256,512,1]{1,0,2:T(8,128)S(1)} fusion(f32[256,512]{1,0:T(8,128)S(1)} %convolution_divide_fusion.1, f32[]{:T(128)} %bitcast.38, f32[]{:T(128)} %bitcast.37, f32[]{:T(128)} %bitcast.36, f32[]{:T(128)} %bitcast.35, f32[]{:T(128)} %bitcast.34, f32[]{:T(128)} %bitcast.33, f32[]{:T(128)} %bitcast.32, f32[]{:T(128)} %bitcast.31, ...), kind=kOutput, calls=%fused_computation.29 | convolution fusion | flops 829947904 | bytes 1048700 | tf_op jit(solution)/shard_map/dot_general | solution.py:70
  184.6 5.3 copy.45
  194.2 104.3 %scatter_fusion = f32[1536,2,512]{2,1,0:T(2,128)} fusion(f32[1536,2,512]{2,1,0:T(2,128)} %broadcast_in_dim.160, s32[1024]{0:T(1024)S(1)} %bitcast.129, f32[1024,2,512]{2,1,0:T(2,128)} %copy.45), kind=kCustom, calls=%fused_computation.5 | custom fusion | bytes 12587008 | tf_op jit(solution)/shard_map/scatter | solution.py:86
  298.5 142.2 %all_to_all.30 = f32[8,192,2,512]{3,2,1,0:T(2,128)} all-to-all(f32[8,192,2,512]{3,2,1,0:T(2,128)} %bitcast.120), channel_id=1, replica_groups=mesh['view'=4,'bx'=2,'by'=4] {'bx','by'}, dimensions={0} | all-to-all | bytes 12582912 | tf_op jit(solution)/shard_map/all_to_all | solution.py:88
  441.0 122.5 %scatter_fusion.1 = f32[256,2,512]{2,1,0:T(2,128)S(1)} fusion(f32[256,2,512]{2,1,0:T(2,128)S(1)} %broadcast_in_dim.158, s32[1536]{0:T(1024)S(1)} %fusion.67, f32[1536,2,512]{2,1,0:T(2,128)} %bitcast.121), kind=kCustom, calls=%fused_computation.6 | custom fusion | flops 1572864 | bytes 18880512 | tf_op jit(solution)/shard_map/scatter-add | solution.py:97
  566.4 34.1 %all-reduce.3.cloned.1.call-done = f32[2,256,512]{2,0,1:T(2,128)} async-done(((f32[2,256,512]{2,0,1:T(2,128)}), f32[2,256,512]{2,0,1:T(2,128)}) %all-reduce.3.cloned.1.call-update) | async-done | bytes 1048592 | tf_op jit(solution)/shard_map/psum | solution.py:106
  604.1 5.0 gather_fusion.2
  609.0 76.9 %all_to_all.31 = f32[8,192,512]{2,1,0:T(8,128)} all-to-all(f32[8,192,512]{2,1,0:T(8,128)} %bitcast.124), channel_id=1, replica_groups=mesh['view'=4,'bx'=2,'by'=4] {'bx','by'}, dimensions={0} | all-to-all | bytes 6291456 | tf_op jit(solution)/shard_map/all_to_all | solution.py:58
  685.9 5.9 gather_fusion.3
  693.5 7.2 fusion.19
  700.7 24.4 %convolution_divide_fusion = f32[256,512]{1,0:T(8,128)S(1)} fusion(f32[256,512]{1,0:T(8,128)S(1)} %fusion.19, f32[1,256,512]{2,1,0:T(8,128)S(1)} %copy-done.6, f32[]{:T(128)} %bitcast.38, f32[]{:T(128)} %bitcast.37, f32[]{:T(128)} %bitcast.36, f32[]{:T(128)} %bitcast.35, f32[]{:T(128)} %bitcast.34, f32[]{:T(128)} %bitcast.33, f32[]{:T(128)} %bitcast.32, ...), kind=kOutput, calls=%fused_computation.24 | convolution fusion | flops 830078976 | bytes 1572988 | tf_op jit(solution)/shard_map/dot_general | solution.py:68
  725.2 24.9 %convolution_bitcast_fusion = f32[256,512,1]{1,0,2:T(8,128)S(1)} fusion(f32[256,512]{1,0:T(8,128)S(1)} %convolution_divide_fusion, f32[]{:T(128)} %bitcast.38, f32[]{:T(128)} %bitcast.37, f32[]{:T(128)} %bitcast.36, f32[]{:T(128)} %bitcast.35, f32[]{:T(128)} %bitcast.34, f32[]{:T(128)} %bitcast.33, f32[]{:T(128)} %bitcast.32, f32[]{:T(128)} %bitcast.31, ...), kind=kOutput, calls=%fused_computation.28 | convolution fusion | flops 829947904 | bytes 1048700 | tf_op jit(solution)/shard_map/dot_general | solution.py:70
  756.9 7.3 scatter_custom_fusion.3
  764.2 74.6 %all_to_all.32 = f32[8,192,1,512]{3,1,2,0:T(8,128)} all-to-all(f32[8,192,1,512]{3,1,2,0:T(8,128)} %bitcast.122), channel_id=1, replica_groups=mesh['view'=4,'bx'=2,'by'=4] {'bx','by'}, dimensions={0} | all-to-all | bytes 6291456 | tf_op jit(solution)/shard_map/all_to_all | solution.py:88
  838.8 11.5 %scatter_custom_fusion.4 = f32[256,512]{1,0:T(8,128)} fusion(s32[1536]{0:T(1024)S(1)} %fusion.67, f32[1536,512]{1,0:T(8,128)} %bitcast.125, f32[]{:T(128)} %constant.37.clone.1), kind=kCustom, calls=%fused_computation.74 | custom fusion | flops 786432 | bytes 524800 | tf_op jit(solution)/shard_map/scatter-add | solution.py:97
  850.3 31.2 %all-reduce.5.cloned.1.call-done = f32[1,256,512]{2,1,0:T(8,128)} async-done(((f32[1,256,512]{2,1,0:T(8,128)}), f32[1,256,512]{2,1,0:T(8,128)}) %all-reduce.5.cloned.1.call-update) | async-done | bytes 524304 | tf_op jit(solution)/shard_map/psum | solution.py:106
  (72 shorter events, 52.8 us)
Async XLA Ops:
  6.5 24.2 %copy-start = (f32[256,512]{1,0:T(8,128)S(1)}, f32[256,512]{1,0:T(8,128)}, u32[]{:S(2)}) copy-start(f32[256,512]{1,0:T(8,128)} %param.6) | copy-start | bytes 1572868
  35.7 4.8 copy-start.7
  35.7 75.0 %all-to-all-start.1 = ((f32[8,192,512]{2,1,0:T(8,128)}), f32[8,192,512]{2,1,0:T(8,128)}, u32[]{:S(2)}, u32[]{:S(2)}) async-start(f32[8,192,512]{2,1,0:T(8,128)} %bitcast.123), calls=%async_computation.1 | async-start | bytes 6291456 | tf_op jit(solution)/shard_map/all_to_all | solution.py:58
  40.3 560.2 %all-reduce.3.cloned.1.call-start = ((), (), s32[]{:S(2)}) async-start(), calls=%async_computation.5 | async-start | bytes 2097152 | tf_op jit(solution)/shard_map/psum | solution.py:106
  118.3 7.2 copy-start.5
  150.0 25.1 %copy-start.1 = (f32[1,4,512,512]{3,2,1,0:T(8,128)S(1)}, f32[1,4,512,512]{3,2,1,0:T(8,128)}, u32[]{:S(2)}) copy-start(f32[1,4,512,512]{3,2,1,0:T(8,128)} %param.8) | copy-start | bytes 12582916
  566.3 315.1 %all-reduce.5.cloned.1.call-start = ((), (), s32[]{:S(2)}) async-start(), calls=%async_computation.6 | async-start | bytes 1048576 | tf_op jit(solution)/shard_map/psum | solution.py:106
  603.1 0.8 copy-start.3
  693.5 7.2 copy-start.6
  725.2 24.9 %copy-start.2 = (f32[1,4,512,512]{3,2,1,0:T(8,128)S(1)}, f32[1,4,512,512]{3,2,1,0:T(8,128)}, u32[]{:S(2)}) copy-start(f32[1,4,512,512]{3,2,1,0:T(8,128)} %param.8) | copy-start | bytes 12582916
  764.2 117.3 %copy-start.4 = (f32[1,256,512]{2,0,1:T(1,128)S(1)}, f32[1,256,512]{2,0,1:T(1,128)}, u32[]{:S(2)}) copy-start(f32[1,256,512]{2,0,1:T(1,128)} %copy-done.3) | copy-start | bytes 1572868
Sparse Core Ops, SparseCore 0:
  566.4 34.0 all-reduce.2
  850.4 30.9 all-reduce.4
where the time goes:
time: 903 us; the launch traced here: 891 us
  blocking collectives  307 us (34%)
  other arithmetic  171 us (19%)
  local copies, waits for them, and re-layouts  164 us (18%)
  matrix products  126 us (14%)
  waiting for transfers between devices  102 us (11%)
  between operations  14 us (2%)
    all_to_all x2, blocking collectives, per_device(): lax.all_to_all(buffer.reshape(peer_count, capacity, layers, column_len),...  217 us
    scatter-add x2, other arithmetic, per_device(): jnp.zeros((columns, layers, column_len), jnp.float32).at[owned_column]  134 us
    scatter x2, local copies, waits for them, and re-layouts, per_device(): buffer = jnp.zeros((peer_count * capacity, layers, column_len), jnp.float...  112 us
    all_to_all x1, blocking collectives, per_device(): lax.all_to_all(outgoing.reshape(peer_count, capacity, column_len), ('bx',...  76.9 us
    psum x2, waiting for transfers between devices, per_device(): view_total = lax.psum(summands, 'view')  65.3 us
    dot_general x2, matrix products, per_device(): smeared = jnp.dot(quotient, blurring.T, precision=precise)  49.9 us
    dot_general x2, matrix products, per_device(): blurred = jnp.dot(forward, blurring, precision=precise)  48.8 us
    all_to_all x1, waiting for transfers between devices, per_device(): lax.all_to_all(outgoing.reshape(peer_count, capacity, column_len), ('bx',...  37 us
  transfers between devices with their start and end apart: 3, of which 3 were waited for; matrix products, arithmetic and copies ran while one was open for 4% of the time, Pallas kernels for 0%

commit v1 on v0

--- a/solution.py
+++ b/solution.py
@@ -5,6 +5,28 @@
 
 ITERS = 2
 precise = lax.Precision.HIGHEST
+
+
+def in_blocks(x, dim, size):
+    before, after = (x.shape[:dim], x.shape[dim + 1 :])
+    return jnp.moveaxis(x.reshape(*before, size, -1, *after), dim, 0)
+
+
+def laid_out(blocks, dim):
+    lengths = list(blocks.shape[1:])
+    lengths[dim] *= blocks.shape[0]
+    return jnp.moveaxis(blocks, 0, dim).reshape(lengths)
+
+
+def swapped_with_each(x, axis, split_dim, concat_dim):
+    size, mine = (lax.axis_size(axis), lax.axis_index(axis))
+    blocks = in_blocks(x, split_dim, size)
+    outs = [blocks[mine]]
+    for step in range(1, size):
+        sent = blocks[mine ^ step]
+        outs.append(lax.ppermute(sent, axis, [(i, i ^ step) for i in range(size)]))
+    blocks = jnp.stack(outs)[mine ^ jnp.arange(size)]
+    return laid_out(blocks, concat_dim)
 
 
 def blur_matrix(taps_row, column_len):
@@ -55,12 +77,8 @@
     norm_local = None
     for sweep in range(ITERS):
         outgoing = estimate[owned_column]
-        incoming = lax.all_to_all(
-            outgoing.reshape(peer_count, capacity, column_len),
-            ("bx", "by"),
-            split_axis=0,
-            concat_axis=0,
-            tiled=True,
+        incoming = swapped_with_each(
+            outgoing.reshape(peer_count, capacity, column_len), ("bx", "by"), 0, 0
         )
         incoming = incoming.reshape(peer_count * capacity, column_len)
         pieces = incoming[position].reshape(columns, sources, column_len)

time: 903 us -> 937 us (1.038)
  blocking collectives: 307 us -> 225 us
  waiting for transfers between devices: 102 us -> 163 us
  starting transfers between devices: 4.83 us -> 32.9 us
  local copies, waits for them, and re-layouts: 164 us -> 191 us
    ppermute x0 -> x14, waiting for transfers between devices: none -> 97.7 us  [swapped_with_each(): outs.append(lax.ppermute(sent, axis, [(i, i ^ step) for i in range(size)]))]
    all_to_all x2 -> x0, blocking collectives: 90.4 us -> none  [the longest x1 76.9 us: per_device(): lax.all_to_all(outgoing.reshape(peer_count, capacity, column_len), ('bx',...]
    all_to_all x1, waiting for transfers between devices: 37 us -> 0.01 us  [per_device(): lax.all_to_all(request.reshape(peer_count, capacity), ('bx', 'by'), split...]
    ppermute x0 -> x14, starting transfers between devices: none -> 25 us  [swapped_with_each(): outs.append(lax.ppermute(sent, axis, [(i, i ^ step) for i in range(size)]))]
  transfers between devices with their start and end apart: 3 -> 17, of which waited for: 3 -> 8; matrix products, arithmetic and copies ran while one was open for 4% -> 5% of each run, Pallas kernels for 0% -> 0%
where the time goes in v1:
time: 937 us; the launch traced here: 925 us
  blocking collectives  225 us (24%)
  local copies, waits for them, and re-layouts  191 us (20%)
  other arithmetic  173 us (18%)
  waiting for transfers between devices  163 us (17%)
  matrix products  126 us (13%)
  starting transfers between devices  32.9 us (4%)
  between operations  13.9 us (1%)
    all_to_all x2, blocking collectives, per_device(): lax.all_to_all(buffer.reshape(peer_count, capacity, layers, column_len),...  225 us
    scatter-add x2, other arithmetic, per_device(): jnp.zeros((columns, layers, column_len), jnp.float32).at[owned_column]  134 us
    scatter x2, local copies, waits for them, and re-layouts, per_device(): buffer = jnp.zeros((peer_count * capacity, layers, column_len), jnp.float...  112 us
    ppermute x14, waiting for transfers between devices, swapped_with_each(): outs.append(lax.ppermute(sent, axis, [(i, i ^ step) for i in range(size)]))  97.7 us
    psum x2, waiting for transfers between devices, per_device(): view_total = lax.psum(summands, 'view')  65 us
    dot_general x2, matrix products, per_device(): smeared = jnp.dot(quotient, blurring.T, precision=precise)  49.4 us
    dot_general x2, matrix products, per_device(): blurred = jnp.dot(forward, blurring, precision=precise)  48.9 us
    ppermute x14, starting transfers between devices, swapped_with_each(): outs.append(lax.ppermute(sent, axis, [(i, i ^ step) for i in range(size)]))  25 us
  transfers between devices with their start and end apart: 17, of which 8 were waited for; matrix products, arithmetic and copies ran while one was open for 5% of the time, Pallas kernels for 0%

profile of v1, /device:TPU:0, one launch (start us, length us, event | category | flops | bytes accessed | tf_op | source)
XLA Modules:
  0.0 924.8 jit_solution(8795130888848241700)
XLA Ops:
  17.6 7.3 all-to-all-start
  29.5 22.7 %fusion.58 = f32[512]{0:T(512)S(1)} fusion(f32[]{:T(128)} %bitcast.54, f32[]{:T(128)} %bitcast.53, f32[]{:T(128)} %bitcast.52, f32[]{:T(128)} %bitcast.51, f32[]{:T(128)} %bitcast.50, f32[]{:T(128)} %bitcast.49, f32[]{:T(128)} %bitcast.48, f32[]{:T(128)} %bitcast.47, f32[]{:T(128)} %bitcast.46, f32[]{:T(128)} %bitcast.45, f32[]{:T(128)} %bitcast.44, ...), kind=kLoop, calls=%fused_computation.75 | loop fusion | flops 24903168 | bytes 2172 | tf_op jit(solution)/shard_map/reduce_sum | solution.py:74
  75.6 10.6 %collective-permute-done = f32[1,192,512]{2,1,0:T(8,128)S(1)} collective-permute-done((f32[1,192,512]{2,1,0:T(8,128)}, f32[1,192,512]{2,1,0:T(8,128)S(1)}, u32[]{:S(2)}, u32[]{:S(2)}) %collective-permute-start) | collective-permute-done | bytes 393248 | tf_op jit(solution)/shard_map/ppermute | solution.py:27
  89.9 8.7 collective-permute-done.1
  105.1 28.2 %collective-permute-done.5 = f32[1,192,512]{2,1,0:T(8,128)S(1)} collective-permute-done((f32[1,192,512]{2,1,0:T(8,128)}, f32[1,192,512]{2,1,0:T(8,128)S(1)}, u32[]{:S(2)}, u32[]{:S(2)}) %collective-permute-start.5) | collective-permute-done | bytes 393248 | tf_op jit(solution)/shard_map/ppermute | solution.py:27
  139.2 5.9 gather_fusion.2
  146.8 7.2 fusion.14
  154.0 24.5 %convolution_divide_fusion.1 = f32[256,512]{1,0:T(8,128)S(1)} fusion(f32[256,512]{1,0:T(8,128)S(1)} %fusion.14, f32[1,256,512]{2,1,0:T(8,128)S(1)} %copy-done.5, f32[]{:T(128)} %bitcast.54, f32[]{:T(128)} %bitcast.53, f32[]{:T(128)} %bitcast.52, f32[]{:T(128)} %bitcast.51, f32[]{:T(128)} %bitcast.50, f32[]{:T(128)} %bitcast.49, f32[]{:T(128)} %bitcast.48, ...), kind=kOutput, calls=%fused_computation.27 | convolution fusion | flops 830078976 | bytes 1572988 | tf_op jit(solution)/shard_map/dot_general | solution.py:86
  178.5 24.6 %convolution_bitcast_fusion.1 = f32[256,512,1]{1,0,2:T(8,128)S(1)} fusion(f32[256,512]{1,0:T(8,128)S(1)} %convolution_divide_fusion.1, f32[]{:T(128)} %bitcast.54, f32[]{:T(128)} %bitcast.53, f32[]{:T(128)} %bitcast.52, f32[]{:T(128)} %bitcast.51, f32[]{:T(128)} %bitcast.50, f32[]{:T(128)} %bitcast.49, f32[]{:T(128)} %bitcast.48, f32[]{:T(128)} %bitcast.47, ...), kind=kOutput, calls=%fused_computation.31 | convolution fusion | flops 829947904 | bytes 1048700 | tf_op jit(solution)/shard_map/dot_general | solution.py:88
  222.3 104.3 %scatter_fusion = f32[1536,2,512]{2,1,0:T(2,128)} fusion(f32[1536,2,512]{2,1,0:T(2,128)} %broadcast_in_dim.162, s32[1024]{0:T(1024)S(1)} %bitcast.191, f32[1024,2,512]{2,1,0:T(2,128)} %copy.45), kind=kCustom, calls=%fused_computation.7 | custom fusion | bytes 12587008 | tf_op jit(solution)/shard_map/scatter | solution.py:104
  326.6 146.5 %all_to_all.19 = f32[8,192,2,512]{3,2,1,0:T(2,128)} all-to-all(f32[8,192,2,512]{3,2,1,0:T(2,128)} %bitcast.181), channel_id=1, replica_groups=mesh['view'=4,'bx'=2,'by'=4] {'bx','by'}, dimensions={0} | all-to-all | bytes 12582912 | tf_op jit(solution)/shard_map/all_to_all | solution.py:106
  473.4 122.5 %scatter_fusion.1 = f32[256,2,512]{2,1,0:T(2,128)S(1)} fusion(f32[256,2,512]{2,1,0:T(2,128)S(1)} %broadcast_in_dim.160, s32[1536]{0:T(1024)S(1)} %fusion.67, f32[1536,2,512]{2,1,0:T(2,128)} %bitcast.182), kind=kCustom, calls=%fused_computation.8 | custom fusion | flops 1572864 | bytes 18880512 | tf_op jit(solution)/shard_map/scatter-add | solution.py:115
  598.7 34.0 %all-reduce.3.cloned.1.call-done = f32[2,256,512]{2,0,1:T(2,128)} async-done(((f32[2,256,512]{2,0,1:T(2,128)}), f32[2,256,512]{2,0,1:T(2,128)}) %all-reduce.3.cloned.1.call-update) | async-done | bytes 1048592 | tf_op jit(solution)/shard_map/psum | solution.py:124
  651.0 13.3 %collective-permute-done.7 = f32[1,192,512]{2,1,0:T(8,128)S(1)} collective-permute-done((f32[1,192,512]{2,1,0:T(8,128)S(1)}, f32[1,192,512]{2,1,0:T(8,128)S(1)}, u32[]{:S(2)}, u32[]{:S(2)}) %collective-permute-start.7) | collective-permute-done | bytes 393248 | tf_op jit(solution)/shard_map/ppermute | solution.py:27
  667.2 8.7 collective-permute-done.8
  682.3 28.2 %collective-permute-done.12 = f32[1,192,512]{2,1,0:T(8,128)S(1)} collective-permute-done((f32[1,192,512]{2,1,0:T(8,128)S(1)}, f32[1,192,512]{2,1,0:T(8,128)S(1)}, u32[]{:S(2)}, u32[]{:S(2)}) %collective-permute-start.12) | collective-permute-done | bytes 393248 | tf_op jit(solution)/shard_map/ppermute | solution.py:27
  716.4 5.9 gather_fusion.5
  724.0 7.2 fusion.19
  731.2 24.3 %convolution_divide_fusion = f32[256,512]{1,0:T(8,128)S(1)} fusion(f32[256,512]{1,0:T(8,128)S(1)} %fusion.19, f32[1,256,512]{2,1,0:T(8,128)S(1)} %copy-done.6, f32[]{:T(128)} %bitcast.54, f32[]{:T(128)} %bitcast.53, f32[]{:T(128)} %bitcast.52, f32[]{:T(128)} %bitcast.51, f32[]{:T(128)} %bitcast.50, f32[]{:T(128)} %bitcast.49, f32[]{:T(128)} %bitcast.48, ...), kind=kOutput, calls=%fused_computation.26 | convolution fusion | flops 830078976 | bytes 1572988 | tf_op jit(solution)/shard_map/dot_general | solution.py:86
  755.6 24.8 %convolution_bitcast_fusion = f32[256,512,1]{1,0,2:T(8,128)S(1)} fusion(f32[256,512]{1,0:T(8,128)S(1)} %convolution_divide_fusion, f32[]{:T(128)} %bitcast.54, f32[]{:T(128)} %bitcast.53, f32[]{:T(128)} %bitcast.52, f32[]{:T(128)} %bitcast.51, f32[]{:T(128)} %bitcast.50, f32[]{:T(128)} %bitcast.49, f32[]{:T(128)} %bitcast.48, f32[]{:T(128)} %bitcast.47, ...), kind=kOutput, calls=%fused_computation.30 | convolution fusion | flops 829947904 | bytes 1048700 | tf_op jit(solution)/shard_map/dot_general | solution.py:88
  787.2 7.3 scatter_custom_fusion.3
  794.5 78.7 %all_to_all.20 = f32[8,192,1,512]{3,1,2,0:T(8,128)} all-to-all(f32[8,192,1,512]{3,1,2,0:T(8,128)} %bitcast.183), channel_id=1, replica_groups=mesh['view'=4,'bx'=2,'by'=4] {'bx','by'}, dimensions={0} | all-to-all | bytes 6291456 | tf_op jit(solution)/shard_map/all_to_all | solution.py:106
  873.2 11.5 %scatter_custom_fusion.4 = f32[256,512]{1,0:T(8,128)} fusion(s32[1536]{0:T(1024)S(1)} %fusion.67, f32[1536,512]{1,0:T(8,128)} %bitcast.187, f32[]{:T(128)} %constant.40.clone.1), kind=kCustom, calls=%fused_computation.106 | custom fusion | flops 786432 | bytes 524800 | tf_op jit(solution)/shard_map/scatter-add | solution.py:115
  884.7 31.0 %all-reduce.5.cloned.1.call-done = f32[1,256,512]{2,1,0:T(8,128)} async-done(((f32[1,256,512]{2,1,0:T(8,128)}), f32[1,256,512]{2,1,0:T(8,128)}) %all-reduce.5.cloned.1.call-update) | async-done | bytes 524304 | tf_op jit(solution)/shard_map/psum | solution.py:124
  (116 shorter events, 122.9 us)
Async XLA Ops:
  6.5 51.6 %copy-start = (f32[256,512]{1,0:T(8,128)S(1)}, f32[256,512]{1,0:T(8,128)}, u32[]{:S(2)}) copy-start(f32[256,512]{1,0:T(8,128)} %param.6) | copy-start | bytes 1572868
  17.6 40.3 %all-to-all-start = ((s32[8,1,192]{2,1,0:T(1,128)}), s32[8,1,192]{2,1,0:T(1,128)S(1)}, u32[]{:S(2)}, u32[]{:S(2)}) async-start(s32[8,1,192]{2,1,0:T(1,128)} %all_to_all.12), calls=%async_computation | async-start | bytes 16384 | tf_op jit(solution)/shard_map/all_to_all | solution.py:67
  24.8 607.9 %all-reduce.3.cloned.1.call-start = ((), (), s32[]{:S(2)}) async-start(), calls=%async_computation.3 | async-start | bytes 2097152 | tf_op jit(solution)/shard_map/psum | solution.py:124
  66.6 19.6 %collective-permute-start = (f32[1,192,512]{2,1,0:T(8,128)}, f32[1,192,512]{2,1,0:T(8,128)S(1)}, u32[]{:S(2)}, u32[]{:S(2)}) collective-permute-start(f32[1,192,512]{2,1,0:T(8,128)} %get-tuple-element.19), channel_id=1, source_target_pairs={{0,1},{1,0},{2,3},{3,2},{4,5},{5,4},{6,7},{7,6},{8,9},{9,8},{10,11... | collective-permute-start | bytes 1179656 | tf_op jit(solution)/shard_map/ppermute | solution.py:27
  68.6 30.1 %collective-permute-start.1 = (f32[1,192,512]{2,1,0:T(8,128)}, f32[1,192,512]{2,1,0:T(8,128)S(1)}, u32[]{:S(2)}, u32[]{:S(2)}) collective-permute-start(f32[1,192,512]{2,1,0:T(8,128)} %get-tuple-element.18), channel_id=1, source_target_pairs={{0,2},{1,3},{2,0},{3,1},{4,6},{5,7},{6,4},{7,5},{8,10},{9,11},{10,... | collective-permute-start | bytes 1179656 | tf_op jit(solution)/shard_map/ppermute | solution.py:27
  73.0 29.7 %collective-permute-start.2 = (f32[1,192,512]{2,1,0:T(8,128)}, f32[1,192,512]{2,1,0:T(8,128)S(1)}, u32[]{:S(2)}, u32[]{:S(2)}) collective-permute-start(f32[1,192,512]{2,1,0:T(8,128)} %get-tuple-element.17), channel_id=1, source_target_pairs={{0,3},{1,2},{2,1},{3,0},{4,7},{5,6},{6,5},{7,4},{8,11},{9,10},{10,... | collective-permute-start | bytes 1179656 | tf_op jit(solution)/shard_map/ppermute | solution.py:27
  73.1 30.4 %collective-permute-start.3 = (f32[1,192,512]{2,1,0:T(8,128)}, f32[1,192,512]{2,1,0:T(8,128)S(1)}, u32[]{:S(2)}, u32[]{:S(2)}) collective-permute-start(f32[1,192,512]{2,1,0:T(8,128)} %get-tuple-element.16), channel_id=1, source_target_pairs={{0,4},{1,5},{2,6},{3,7},{4,0},{5,1},{6,2},{7,3},{8,12},{9,13},{10,... | collective-permute-start | bytes 1179656 | tf_op jit(solution)/shard_map/ppermute | solution.py:27
  75.0 29.3 %collective-permute-start.4 = (f32[1,192,512]{2,1,0:T(8,128)}, f32[1,192,512]{2,1,0:T(8,128)S(1)}, u32[]{:S(2)}, u32[]{:S(2)}) collective-permute-start(f32[1,192,512]{2,1,0:T(8,128)} %get-tuple-element.15), channel_id=1, source_target_pairs={{0,5},{1,4},{2,7},{3,6},{4,1},{5,0},{6,3},{7,2},{8,13},{9,12},{10,... | collective-permute-start | bytes 1179656 | tf_op jit(solution)/shard_map/ppermute | solution.py:27
  86.2 47.1 %collective-permute-start.5 = (f32[1,192,512]{2,1,0:T(8,128)}, f32[1,192,512]{2,1,0:T(8,128)S(1)}, u32[]{:S(2)}, u32[]{:S(2)}) collective-permute-start(f32[1,192,512]{2,1,0:T(8,128)} %get-tuple-element.14), channel_id=1, source_target_pairs={{0,6},{1,7},{2,4},{3,5},{4,2},{5,3},{6,0},{7,1},{8,14},{9,15},{10,... | collective-permute-start | bytes 1179656 | tf_op jit(solution)/shard_map/ppermute | solution.py:27
  98.7 35.4 %collective-permute-start.6 = (f32[1,192,512]{2,1,0:T(8,128)}, f32[1,192,512]{2,1,0:T(8,128)S(1)}, u32[]{:S(2)}, u32[]{:S(2)}) collective-permute-start(f32[1,192,512]{2,1,0:T(8,128)} %get-tuple-element.13), channel_id=1, source_target_pairs={{0,7},{1,6},{2,5},{3,4},{4,3},{5,2},{6,1},{7,0},{8,15},{9,14},{10,... | collective-permute-start | bytes 1179656 | tf_op jit(solution)/shard_map/ppermute | solution.py:27
  146.7 7.2 copy-start.5
  178.5 24.6 %copy-start.1 = (f32[1,4,512,512]{3,2,1,0:T(8,128)S(1)}, f32[1,4,512,512]{3,2,1,0:T(8,128)}, u32[]{:S(2)}) copy-start(f32[1,4,512,512]{3,2,1,0:T(8,128)} %param.8) | copy-start | bytes 12582916
  598.7 317.0 %all-reduce.5.cloned.1.call-start = ((), (), s32[]{:S(2)}) async-start(), calls=%async_computation.4 | async-start | bytes 1048576 | tf_op jit(solution)/shard_map/psum | solution.py:124
  635.3 0.8 copy-start.3
  644.5 19.7 %collective-permute-start.7 = (f32[1,192,512]{2,1,0:T(8,128)S(1)}, f32[1,192,512]{2,1,0:T(8,128)S(1)}, u32[]{:S(2)}, u32[]{:S(2)}) collective-permute-start(f32[1,192,512]{2,1,0:T(8,128)S(1)} %get-tuple-element.11), channel_id=1, source_target_pairs={{0,1},{1,0},{2,3},{3,2},{4,5},{5,4},{6,7},{7,6},{8,9},{9,8},{10,11... | collective-permute-start | bytes 1179656 | tf_op jit(solution)/shard_map/ppermute | solution.py:27
  646.0 29.8 %collective-permute-start.8 = (f32[1,192,512]{2,1,0:T(8,128)S(1)}, f32[1,192,512]{2,1,0:T(8,128)S(1)}, u32[]{:S(2)}, u32[]{:S(2)}) collective-permute-start(f32[1,192,512]{2,1,0:T(8,128)S(1)} %get-tuple-element.10), channel_id=1, source_target_pairs={{0,2},{1,3},{2,0},{3,1},{4,6},{5,7},{6,4},{7,5},{8,10},{9,11},{10,... | collective-permute-start | bytes 1179656 | tf_op jit(solution)/shard_map/ppermute | solution.py:27
  648.4 31.5 %collective-permute-start.9 = (f32[1,192,512]{2,1,0:T(8,128)S(1)}, f32[1,192,512]{2,1,0:T(8,128)S(1)}, u32[]{:S(2)}, u32[]{:S(2)}) collective-permute-start(f32[1,192,512]{2,1,0:T(8,128)S(1)} %get-tuple-element.9), channel_id=1, source_target_pairs={{0,3},{1,2},{2,1},{3,0},{4,7},{5,6},{6,5},{7,4},{8,11},{9,10},{10,... | collective-permute-start | bytes 1179656 | tf_op jit(solution)/shard_map/ppermute | solution.py:27
  648.9 31.8 %collective-permute-start.10 = (f32[1,192,512]{2,1,0:T(8,128)S(1)}, f32[1,192,512]{2,1,0:T(8,128)S(1)}, u32[]{:S(2)}, u32[]{:S(2)}) collective-permute-start(f32[1,192,512]{2,1,0:T(8,128)S(1)} %get-tuple-element.8), channel_id=1, source_target_pairs={{0,4},{1,5},{2,6},{3,7},{4,0},{5,1},{6,2},{7,3},{8,12},{9,13},{10,... | collective-permute-start | bytes 1179656 | tf_op jit(solution)/shard_map/ppermute | solution.py:27
  650.4 31.1 %collective-permute-start.11 = (f32[1,192,512]{2,1,0:T(8,128)S(1)}, f32[1,192,512]{2,1,0:T(8,128)S(1)}, u32[]{:S(2)}, u32[]{:S(2)}) collective-permute-start(f32[1,192,512]{2,1,0:T(8,128)S(1)} %get-tuple-element.7), channel_id=1, source_target_pairs={{0,5},{1,4},{2,7},{3,6},{4,1},{5,0},{6,3},{7,2},{8,13},{9,12},{10,... | collective-permute-start | bytes 1179656 | tf_op jit(solution)/shard_map/ppermute | solution.py:27
  664.2 46.2 %collective-permute-start.12 = (f32[1,192,512]{2,1,0:T(8,128)S(1)}, f32[1,192,512]{2,1,0:T(8,128)S(1)}, u32[]{:S(2)}, u32[]{:S(2)}) collective-permute-start(f32[1,192,512]{2,1,0:T(8,128)S(1)} %get-tuple-element.6), channel_id=1, source_target_pairs={{0,6},{1,7},{2,4},{3,5},{4,2},{5,3},{6,0},{7,1},{8,14},{9,15},{10,... | collective-permute-start | bytes 1179656 | tf_op jit(solution)/shard_map/ppermute | solution.py:27
  675.9 35.4 %collective-permute-start.13 = (f32[1,192,512]{2,1,0:T(8,128)S(1)}, f32[1,192,512]{2,1,0:T(8,128)S(1)}, u32[]{:S(2)}, u32[]{:S(2)}) collective-permute-start(f32[1,192,512]{2,1,0:T(8,128)S(1)} %get-tuple-element.5), channel_id=1, source_target_pairs={{0,7},{1,6},{2,5},{3,4},{4,3},{5,2},{6,1},{7,0},{8,15},{9,14},{10,... | collective-permute-start | bytes 1179656 | tf_op jit(solution)/shard_map/ppermute | solution.py:27
  724.0 7.2 copy-start.6
  755.6 24.8 %copy-start.2 = (f32[1,4,512,512]{3,2,1,0:T(8,128)S(1)}, f32[1,4,512,512]{3,2,1,0:T(8,128)}, u32[]{:S(2)}) copy-start(f32[1,4,512,512]{3,2,1,0:T(8,128)} %param.8) | copy-start | bytes 12582916
  794.5 121.2 %copy-start.4 = (f32[1,256,512]{2,0,1:T(1,128)S(1)}, f32[1,256,512]{2,0,1:T(1,128)}, u32[]{:S(2)}) copy-start(f32[1,256,512]{2,0,1:T(1,128)} %copy-done.3) | copy-start | bytes 1572868
Sparse Core Ops, SparseCore 0:
  598.8 33.9 all-reduce.2
  884.8 30.8 all-reduce.4
